TPU v7x, 32 devices: a whole 2x2x4 slice. The times are simulated.
32 devices in a mesh: hot: 4 (over y, x), tt: 8 (over z, core).
Axes of the slice: x: 2, y: 2, z: 4, core: 2. Of those that a mesh axis runs over, the one named last changes fastest.
Arguments:
- hot_table: float32 [1024, 256], P('hot'), may hold values from -1.5 to 1.5
- hot_accum: float32 [1024], P('hot'), may hold values from 0.05 to 1
- hot_owner: int32 [8192, 1], P(('hot', 'tt')), may hold values from 0 to 3; in each aligned block of 256 rows (0 to 255, 256 to 511, ...) at most 128 rows name the same one
- hot_row: int32 [32, 256], P(('hot', 'tt')), may hold values from 0 to 255
- hot_bag: int32 [32, 256], P(('hot', 'tt')), may hold values from 0 to 63, never falling along the last dimension, each value on 1 to 12 neighbouring positions
- cold_owner: int32 [16384, 1], P(('hot', 'tt')), may hold values from 0 to 7; in each aligned block of 512 rows (0 to 511, 512 to 1023, ...) at most 128 rows name the same one
- first_index: int32 [32, 512], P(('hot', 'tt')), may hold values from 0 to 127
- mid_index: int32 [32, 512], P(('hot', 'tt')), may hold values from 0 to 63
- last_index: int32 [32, 512], P(('hot', 'tt')), may hold values from 0 to 63
- cold_bag: int32 [32, 512], P(('hot', 'tt')), may hold values from 0 to 63, never falling along the last dimension, each value on 1 to 24 neighbouring positions
- core_first: float32 [1024, 256], P('tt'), may hold values from -1 to 1
- core_mid: bfloat16 [64, 8192], replicated, may hold values from -1 to 1
- core_last: bfloat16 [64, 128], replicated, may hold values from -6 to 6
- bag_grads: bfloat16 [2048, 256], P(('hot', 'tt')), may hold values from -6 to 6
Outputs:
- pooled: float32 [2048, 256], P(('hot', 'tt'))
- new_table: float32 [1024, 256], P('hot')
- new_accum: float32 [1024], P('hot')
- new_first: float32 [1024, 256], P('tt')
Inputs may be any that keep to these rules, and one draw needn't show every extreme that they name: `hot_owner`: among the 256 hot lookups of one device no owner appears more than 128 times; some owner appears exactly that often. `cold_owner`: among the 512 cold lookups of one device no owner appears more than 128 times; some owner appears exactly that often. `hot_bag`: never falling along a device's lookups; every bag of a device has at least one hot lookup. `cold_bag`: never falling along a device's lookups; every bag of a device has at least one cold lookup.
All inputs are finite; a program needn't handle non-finite values.
Results may differ from a plain program's by a relative error of at most 0.005.
Values may be sent and summed in bfloat16 or wider, within the bound.
No kernel may reach another device: no remote copies, remote signals or barrier semaphores. Data moves between devices by JAX's collectives and lax.ppermute only.
A program may use at most 64 MiB of HBM per device.

v0:
```python
import math
import jax
import jax.numpy as jnp
from jax import lax
from jax.sharding import PartitionSpec as P

E1 = 8
E2 = 8
E3 = 4
RANK = 32


def slots_of(owners, peer_count):
    chosen = (owners[:, None] == jnp.arange(peer_count, dtype=jnp.int32)[None, :]).astype(jnp.int32)
    before = jnp.cumsum(chosen, axis=0) - chosen
    return jnp.sum(before * chosen, axis=1)


def slot_source(slot_keys, total_slots):
    lookups = slot_keys.shape[0]
    empty = jnp.full((total_slots,), lookups, jnp.int32)
    return empty.at[slot_keys].set(jnp.arange(lookups, dtype=jnp.int32))


def packed(values, source, fill_value):
    return jnp.take(values, source, axis=0, mode="fill", fill_value=fill_value)


def owner_sum(targets, values, held, precision):
    block_rows = math.gcd(held, 512)
    starts = jnp.arange(held // block_rows, dtype=jnp.int32) * block_rows
    offsets = jnp.arange(block_rows, dtype=jnp.int32)

    def owner_one_block(start):
        picks = ((start + offsets)[:, None] == targets[None, :]).astype(values.dtype)
        return jnp.dot(picks, values, precision=precision, preferred_element_type=jnp.float32)

    return lax.map(owner_one_block, starts).reshape(held, values.shape[1])


def adagrad(table_part, accum_part, grad_part):
    accum_next = accum_part + jnp.mean(grad_part * grad_part, axis=1)
    return (table_part - 0.1 * grad_part / (jnp.sqrt(accum_next)[:, None] + 1e-08), accum_next)


def rank_maps(core_mid, core_last, middle, lasts):
    lookups = middle.shape[0]
    block_rows = math.gcd(lookups, 128)

    def rank_one_block(indices):
        mid_part, last_part = indices
        mid_cores = core_mid[mid_part].reshape(-1, RANK, E2, RANK)
        last_cores = core_last[last_part].reshape(-1, RANK, E3)
        made = jnp.einsum(
            "nawb,nbe->nawe", mid_cores, last_cores, preferred_element_type=jnp.float32
        )
        return made.astype(jnp.bfloat16).reshape(-1, RANK * E2 * E3)

    blocks = lax.map(
        rank_one_block, (middle.reshape(-1, block_rows), lasts.reshape(-1, block_rows))
    )
    return blocks.reshape(lookups, RANK * E2 * E3)


def local(
    hot_table,
    hot_accum,
    hot_owner,
    hot_row,
    hot_bag,
    cold_owner,
    first_index,
    mid_index,
    last_index,
    cold_bag,
    core_first,
    core_mid,
    core_last,
    bag_grads,
):
    rows_held = hot_table.shape[0]
    feature_width = hot_table.shape[1]
    tail_width = feature_width // E1
    bag_count = bag_grads.shape[0]
    bag_range = jnp.arange(bag_count, dtype=jnp.int32)
    hot_peers = lax.axis_size("hot")
    hot_lookups = hot_owner.shape[0]
    hot_cap = 2 * hot_lookups // hot_peers
    row_owner = hot_owner[:, 0]
    row_key = row_owner * hot_cap + slots_of(row_owner, hot_peers)
    row_source = slot_source(row_key, hot_peers * hot_cap)
    request = packed(hot_row[0], row_source, -1).reshape(hot_peers, hot_cap)
    wanted = lax.all_to_all(request, "hot", split_axis=0, concat_axis=0, tiled=True)
    picked = hot_table[jnp.maximum(wanted, 0)].astype(jnp.bfloat16)
    replies = lax.all_to_all(picked, "hot", split_axis=0, concat_axis=0, tiled=True)
    served = wanted
    hot_rows = replies.reshape(-1, feature_width)[row_key]
    hot_pick = (hot_bag[0][:, None] == bag_range[None, :]).astype(jnp.bfloat16)
    hot_cot = jnp.dot(hot_pick, bag_grads, preferred_element_type=jnp.float32).astype(jnp.bfloat16)
    sending = packed(hot_cot, row_source, 0).reshape(hot_peers, hot_cap, feature_width)
    received = lax.all_to_all(sending, "hot", split_axis=0, concat_axis=0, tiled=True)
    row_grad = owner_sum(served.reshape(-1), received.reshape(-1, feature_width), rows_held, None)
    total_grad = lax.psum(row_grad, "tt")
    new_table, new_accum = adagrad(hot_table, hot_accum, total_grad)
    slices_held = core_first.shape[0]
    tt_peers = lax.axis_size("tt")
    cold_lookups = cold_owner.shape[0]
    cold_cap = 2 * cold_lookups // tt_peers
    slice_owner = cold_owner[:, 0]
    slice_key = slice_owner * cold_cap + slots_of(slice_owner, tt_peers)
    slice_source = slot_source(slice_key, tt_peers * cold_cap)
    maps = rank_maps(core_mid, core_last, mid_index[0], last_index[0])
    cold_pick = (cold_bag[0][:, None] == bag_range[None, :]).astype(jnp.bfloat16)
    cold_cot = jnp.dot(cold_pick, bag_grads, preferred_element_type=jnp.float32).astype(
        jnp.bfloat16
    )
    slice_request = packed(first_index[0], slice_source, -1).reshape(tt_peers, cold_cap)
    wanted = lax.all_to_all(slice_request, "tt", split_axis=0, concat_axis=0, tiled=True)
    slices = core_first[jnp.maximum(wanted, 0)].astype(jnp.bfloat16)
    back = lax.all_to_all(slices, "tt", split_axis=0, concat_axis=0, tiled=True)
    slices = back.reshape(-1, E1 * RANK)[slice_key].reshape(cold_lookups, E1, RANK)
    maps_three = maps.reshape(cold_lookups, RANK, tail_width)
    cold_rows = jnp.einsum("kea,kaj->kej", slices, maps_three, preferred_element_type=jnp.float32)
    cold_rows = cold_rows.astype(jnp.bfloat16).reshape(cold_lookups, feature_width)
    local_terms = jnp.einsum(
        "kej,kaj->kea",
        cold_cot.reshape(cold_lookups, E1, tail_width),
        maps_three,
        preferred_element_type=jnp.float32,
    )
    grad_out = packed(local_terms.reshape(cold_lookups, E1 * RANK), slice_source, 0).reshape(
        tt_peers, cold_cap, E1 * RANK
    )
    terms = lax.all_to_all(grad_out, "tt", split_axis=0, concat_axis=0, tiled=True).reshape(
        -1, E1 * RANK
    )
    core_grad = owner_sum(wanted.reshape(-1), terms, slices_held, lax.Precision.HIGHEST)
    core_total = lax.psum(core_grad, "hot")
    new_first = core_first - 0.01 * core_total
    all_rows = jnp.concatenate([hot_rows, cold_rows], axis=0)
    all_picks = jnp.concatenate([hot_pick, cold_pick], axis=0)
    pooled = jnp.einsum("lb,le->be", all_picks, all_rows, preferred_element_type=jnp.float32)
    return (pooled, new_table, new_accum, new_first)


def solution(mesh):
    placed = (
        P("hot", None),
        P("hot"),
        P(("hot", "tt"), None),
        P(("hot", "tt"), None),
        P(("hot", "tt"), None),
        P(("hot", "tt"), None),
        P(("hot", "tt"), None),
        P(("hot", "tt"), None),
        P(("hot", "tt"), None),
        P(("hot", "tt"), None),
        P("tt", None),
        P(),
        P(),
        P(("hot", "tt"), None),
    )
    return jax.shard_map(
        local,
        mesh=mesh,
        in_specs=placed,
        out_specs=(P(("hot", "tt"), None), P("hot", None), P("hot"), P("tt", None)),
        check_vma=False,
    )
```

profile of v0, /device:TPU:0, one launch (start us, length us, event | category | flops | bytes accessed | tf_op | source)
XLA Modules:
  0.0 373.3 jit_solution(5396923980867032876)
XLA Ops:
  8.7 1.2 reduce-window.14
  11.7 1.4 scatter_custom_fusion
  13.1 3.6 gather_fusion.2
  17.3 5.2 %all-to-all-start = ((s32[4,1,128]{2,1,0:T(1,128)}), s32[4,1,128]{2,1,0:T(1,128)S(1)}, u32[]{:S(2)}, u32[]{:S(2)}) async-start(s32[4,1,128]{2,1,0:T(1,128)} %bitcast.17), calls=%async_computation | async-start | bytes 4096 | tf_op jit(solution)/shard_map/all_to_all | solution.py:93
  26.1 2.6 scatter_custom_fusion.1
  28.7 154.8 %while.2 = (s32[]{:T(128)}, bf16[4,128,1024]{2,1,0:T(8,128)(2,1)S(1)}, s32[4,128]{1,0:T(4,128)}, bf16[64,8192]{1,0:T(8,128)(2,1)}, s32[4,128]{1,0:T(4,128)}, /*index=5*/bf16[64,128]{1,0:T(8,128)(2,1)}, s32[]{:T(128)}) while((s32[]{:T(128)}, bf16[4,128,1024]{2,1,0:T(8,128)(2,1)S(1)}, s32[4,128]{1,0:T(4,128)}, bf16[64,8192]{1,0:T(8,128)(2,1)}, ...), condition=%wide.region_9.10_spmd, body=%wide.region_8.9_spmd.sunk | while | flops 8522498 | bytes 16822392 | solution.py:59
  29.4 6.5 %gather_fusion = bf16[128,8192]{1,0:T(8,128)(2,1)} fusion(bf16[64,8192]{1,0:T(8,128)(2,1)} %get-tuple-element.145, s32[1024]{0:T(1024)S(1)} %pad_clamp_fusion.8), kind=kCustom, calls=%fused_computation.clone.1 | custom fusion | bytes 4194816 | tf_op jit(solution)/shard_map/while/body/eval_jaxpr/gather | solution.py:52
  35.9 3.2 copy.55
  39.2 11.7 %copy.56 = bf16[128,32,8,32]{3,1,2,0:T(8,128)(2,1)} copy(bf16[128,32,8,32]{0,3,2,1:T(8,128)(2,1)S(1)} %bitcast.108) | data formatting | bytes 4194304 | tf_op jit(solution)/shard_map/while/body/eval_jaxpr/reshape | solution.py:52
  51.9 14.3 %convolution_convert_fusion.5 = bf16[128,32,8,4]{1,3,2,0:T(4,128)(2,1)S(1)} fusion(bf16[128,32,8,32]{3,1,2,0:T(8,128)(2,1)} %copy.56, bf16[128,32,4,1]{1,2,3,0:T(4,128)(2,1)S(1)} %copy.58), kind=kOutput, calls=%fused_computation.12.clone.1 | convolution fusion | flops 8519680 | bytes 2392064 | tf_op jit(solution)/shard_map/while/body/eval_jaxpr/nawb,nbe->nawe/dot_general | solution.py:54
  68.1 6.5 %gather_fusion = bf16[128,8192]{1,0:T(8,128)(2,1)} fusion(bf16[64,8192]{1,0:T(8,128)(2,1)} %get-tuple-element.145, s32[1024]{0:T(1024)S(1)} %pad_clamp_fusion.8), kind=kCustom, calls=%fused_computation.clone.1 | custom fusion | bytes 4194816 | tf_op jit(solution)/shard_map/while/body/eval_jaxpr/gather | solution.py:52
  74.6 3.2 copy.55
  77.8 11.7 %copy.56 = bf16[128,32,8,32]{3,1,2,0:T(8,128)(2,1)} copy(bf16[128,32,8,32]{0,3,2,1:T(8,128)(2,1)S(1)} %bitcast.108) | data formatting | bytes 4194304 | tf_op jit(solution)/shard_map/while/body/eval_jaxpr/reshape | solution.py:52
  90.6 14.3 %convolution_convert_fusion.5 = bf16[128,32,8,4]{1,3,2,0:T(4,128)(2,1)S(1)} fusion(bf16[128,32,8,32]{3,1,2,0:T(8,128)(2,1)} %copy.56, bf16[128,32,4,1]{1,2,3,0:T(4,128)(2,1)S(1)} %copy.58), kind=kOutput, calls=%fused_computation.12.clone.1 | convolution fusion | flops 8519680 | bytes 2392064 | tf_op jit(solution)/shard_map/while/body/eval_jaxpr/nawb,nbe->nawe/dot_general | solution.py:54
  106.8 6.5 %gather_fusion = bf16[128,8192]{1,0:T(8,128)(2,1)} fusion(bf16[64,8192]{1,0:T(8,128)(2,1)} %get-tuple-element.145, s32[1024]{0:T(1024)S(1)} %pad_clamp_fusion.8), kind=kCustom, calls=%fused_computation.clone.1 | custom fusion | bytes 4194816 | tf_op jit(solution)/shard_map/while/body/eval_jaxpr/gather | solution.py:52
  113.3 3.2 copy.55
  116.5 11.7 %copy.56 = bf16[128,32,8,32]{3,1,2,0:T(8,128)(2,1)} copy(bf16[128,32,8,32]{0,3,2,1:T(8,128)(2,1)S(1)} %bitcast.108) | data formatting | bytes 4194304 | tf_op jit(solution)/shard_map/while/body/eval_jaxpr/reshape | solution.py:52
  129.3 14.3 %convolution_convert_fusion.5 = bf16[128,32,8,4]{1,3,2,0:T(4,128)(2,1)S(1)} fusion(bf16[128,32,8,32]{3,1,2,0:T(8,128)(2,1)} %copy.56, bf16[128,32,4,1]{1,2,3,0:T(4,128)(2,1)S(1)} %copy.58), kind=kOutput, calls=%fused_computation.12.clone.1 | convolution fusion | flops 8519680 | bytes 2392064 | tf_op jit(solution)/shard_map/while/body/eval_jaxpr/nawb,nbe->nawe/dot_general | solution.py:54
  145.5 6.5 %gather_fusion = bf16[128,8192]{1,0:T(8,128)(2,1)} fusion(bf16[64,8192]{1,0:T(8,128)(2,1)} %get-tuple-element.145, s32[1024]{0:T(1024)S(1)} %pad_clamp_fusion.8), kind=kCustom, calls=%fused_computation.clone.1 | custom fusion | bytes 4194816 | tf_op jit(solution)/shard_map/while/body/eval_jaxpr/gather | solution.py:52
  152.0 3.2 copy.55
  155.2 11.7 %copy.56 = bf16[128,32,8,32]{3,1,2,0:T(8,128)(2,1)} copy(bf16[128,32,8,32]{0,3,2,1:T(8,128)(2,1)S(1)} %bitcast.108) | data formatting | bytes 4194304 | tf_op jit(solution)/shard_map/while/body/eval_jaxpr/reshape | solution.py:52
  168.0 14.3 %convolution_convert_fusion.5 = bf16[128,32,8,4]{1,3,2,0:T(4,128)(2,1)S(1)} fusion(bf16[128,32,8,32]{3,1,2,0:T(8,128)(2,1)} %copy.56, bf16[128,32,4,1]{1,2,3,0:T(4,128)(2,1)S(1)} %copy.58), kind=kOutput, calls=%fused_computation.12.clone.1 | convolution fusion | flops 8519680 | bytes 2392064 | tf_op jit(solution)/shard_map/while/body/eval_jaxpr/nawb,nbe->nawe/dot_general | solution.py:54
  183.8 2.0 gather_fusion.8
  185.8 6.9 %gather_fusion.5 = s32[1024]{0:T(1024)S(1)} fusion(s32[512]{0:T(512)S(1)} %bitcast.106, s32[1024]{0:T(1024)S(1)} %fusion.18), kind=kCustom, calls=%fused_computation.5 | custom fusion | bytes 12288 | tf_op jit(solution)/shard_map/jit(_take)/gather | solution.py:26
  194.1 4.4 %reshape.359 = bf16[512,32,32]{2,1,0:T(8,128)(2,1)} reshape(bf16[4,128,1024]{2,1,0:T(8,128)(2,1)S(1)} %get-tuple-element.66) | data formatting | bytes 2097152 | tf_op jit(solution)/shard_map/reshape;reshape | solution.py:122
  198.4 4.9 %all-to-all-start.2 = ((s32[8,1,128]{2,1,0:T(1,128)}), s32[8,1,128]{2,1,0:T(1,128)S(1)}, u32[]{:S(2)}, u32[]{:S(2)}) async-start(s32[8,1,128]{2,1,0:T(1,128)} %bitcast.28), calls=%async_computation.2 | async-start | bytes 8192 | tf_op jit(solution)/shard_map/all_to_all | solution.py:118
  203.3 2.2 gather_fusion.3
  205.5 3.3 all-to-all-done.2
  208.8 4.2 %all-to-all-start.4 = ((bf16[4,128,256]{2,1,0:T(8,128)(2,1)}), bf16[4,128,256]{2,1,0:T(8,128)(2,1)S(1)}, u32[]{:S(2)}, u32[]{:S(2)}) async-start(bf16[4,128,256]{2,1,0:T(8,128)(2,1)} %broadcast_select_fusion.1), calls=%async_computation.4 | async-start | bytes 524288 | tf_op jit(solution)/shard_map/all_to_all | solution.py:101
  213.0 5.4 %all-to-all-done.4 = bf16[4,128,256]{2,1,0:T(8,128)(2,1)S(1)} async-done(((bf16[4,128,256]{2,1,0:T(8,128)(2,1)}), bf16[4,128,256]{2,1,0:T(8,128)(2,1)S(1)}, u32[]{:S(2)}, u32[]{:S(2)}) %all-to-all-start.4) | async-done | bytes 262176 | tf_op jit(solution)/shard_map/all_to_all | solution.py:101
  218.4 3.4 all-to-all-start.1
  221.8 4.6 %gather_fusion.6 = bf16[1024,256]{1,0:T(8,128)(2,1)} fusion(f32[128,256]{1,0:T(8,128)S(1)} %copy-done.2, s32[1024]{0:T(1024)S(1)} %broadcast_clamp_fusion), kind=kCustom, calls=%fused_computation.6 | custom fusion | bytes 1052672 | tf_op jit(solution)/shard_map/gather | solution.py:119
  227.1 3.5 all-to-all-start.3
  231.0 1.7 copy.36
  232.7 4.8 %fusion.25 = f32[512,8,32]{2,1,0:T(8,128)S(1)} fusion(bf16[512,8,32]{2,1,0:T(8,128)(2,1)} %copy.36, bf16[512,32,32]{2,1,0:T(8,128)(2,1)} %reshape.359), kind=kOutput, calls=%fused_computation.83 | convolution fusion | flops 8388608 | bytes 1835008 | tf_op jit(solution)/shard_map/kej,kaj->kea/dot_general | solution.py:125
  237.4 1.5 copy.38
  238.9 1.2 copy.39
  240.2 3.5 gather_fusion.9
  243.7 1.2 broadcast_select_fusion
  245.9 4.0 %all-to-all-start.5 = ((f32[8,128,256]{2,1,0:T(8,128)}), f32[8,128,256]{2,1,0:T(8,128)S(1)}, u32[]{:S(2)}, u32[]{:S(2)}) async-start(f32[8,128,256]{2,1,0:T(8,128)} %broadcast_select_fusion), calls=%async_computation.5 | async-start | bytes 2097152 | tf_op jit(solution)/shard_map/all_to_all | solution.py:134
  251.2 1.2 gather_fusion.4
  252.5 63.3 %all-reduce.3.cloned.1.call-done = f32[256,256]{1,0:T(8,128)} async-done(((f32[256,256]{1,0:T(8,128)}), f32[256,256]{1,0:T(8,128)}) %all-reduce.3.cloned.1.call-update) | async-done | bytes 262160 | tf_op jit(solution)/shard_map/psum | solution.py:103
  317.5 1.8 divide_subtract_fusion
  319.2 1.9 gather_fusion.7
  322.1 1.2 fusion.5
  323.4 3.4 convolution_convert_fusion.1
  328.4 35.9 %all-reduce.5.cloned.1.call-done = f32[128,256]{1,0:T(8,128)} async-done(((f32[128,256]{1,0:T(8,128)}), f32[128,256]{1,0:T(8,128)}) %all-reduce.5.cloned.1.call-update) | async-done | bytes 131088 | tf_op jit(solution)/shard_map/psum | solution.py:138
  364.2 1.6 multiply_subtract_fusion
  (113 shorter events, 27.8 us)
Async XLA Ops:
  8.0 175.5 %copy-start = (bf16[64,256]{1,0:T(8,128)(2,1)S(1)}, bf16[64,256]{1,0:T(8,128)(2,1)}, u32[]{:S(2)}) copy-start(bf16[64,256]{1,0:T(8,128)(2,1)} %param.29) | copy-start | bytes 98308
  17.3 181.1 %all-to-all-start = ((s32[4,1,128]{2,1,0:T(1,128)}), s32[4,1,128]{2,1,0:T(1,128)S(1)}, u32[]{:S(2)}, u32[]{:S(2)}) async-start(s32[4,1,128]{2,1,0:T(1,128)} %bitcast.17), calls=%async_computation | async-start | bytes 4096 | tf_op jit(solution)/shard_map/all_to_all | solution.py:93
  28.7 154.8 %copy-start.8 = (s32[1,256]{1,0:T(1,128)S(1)}, s32[1,256]{1,0:T(1,128)}, u32[]{:S(2)}) copy-start(s32[1,256]{1,0:T(1,128)} %param.20) | copy-start | bytes 3076
  39.1 11.7 %copy-start.3 = (bf16[64,128]{1,0:T(8,128)(2,1)S(1)}, bf16[64,128]{1,0:T(8,128)(2,1)}, u32[]{:S(2)}) copy-start(bf16[64,128]{1,0:T(8,128)(2,1)} %get-tuple-element.147) | copy-start | bytes 49156 | tf_op jit(solution)/shard_map/while
  77.8 11.7 %copy-start.3 = (bf16[64,128]{1,0:T(8,128)(2,1)S(1)}, bf16[64,128]{1,0:T(8,128)(2,1)}, u32[]{:S(2)}) copy-start(bf16[64,128]{1,0:T(8,128)(2,1)} %get-tuple-element.147) | copy-start | bytes 49156 | tf_op jit(solution)/shard_map/while
  116.5 11.7 %copy-start.3 = (bf16[64,128]{1,0:T(8,128)(2,1)S(1)}, bf16[64,128]{1,0:T(8,128)(2,1)}, u32[]{:S(2)}) copy-start(bf16[64,128]{1,0:T(8,128)(2,1)} %get-tuple-element.147) | copy-start | bytes 49156 | tf_op jit(solution)/shard_map/while
  155.2 11.7 %copy-start.3 = (bf16[64,128]{1,0:T(8,128)(2,1)S(1)}, bf16[64,128]{1,0:T(8,128)(2,1)}, u32[]{:S(2)}) copy-start(bf16[64,128]{1,0:T(8,128)(2,1)} %get-tuple-element.147) | copy-start | bytes 49156 | tf_op jit(solution)/shard_map/while
  183.5 2.2 copy-start.1
  185.7 17.6 %copy-start.4 = (f32[256,256]{1,0:T(8,128)S(1)}, f32[256,256]{1,0:T(8,128)}, u32[]{:S(2)}) copy-start(f32[256,256]{1,0:T(8,128)} %param.16) | copy-start | bytes 786436
  194.1 27.7 %copy-start.2 = (f32[128,256]{1,0:T(8,128)S(1)}, f32[128,256]{1,0:T(8,128)}, u32[]{:S(2)}) copy-start(f32[128,256]{1,0:T(8,128)} %param.26) | copy-start | bytes 393220
  198.4 10.4 %all-to-all-start.2 = ((s32[8,1,128]{2,1,0:T(1,128)}), s32[8,1,128]{2,1,0:T(1,128)S(1)}, u32[]{:S(2)}, u32[]{:S(2)}) async-start(s32[8,1,128]{2,1,0:T(1,128)} %bitcast.28), calls=%async_computation.2 | async-start | bytes 8192 | tf_op jit(solution)/shard_map/all_to_all | solution.py:118
  203.3 27.3 %copy-start.7 = (s32[1,512]{1,0:T(1,128)S(1)}, s32[1,512]{1,0:T(1,128)}, u32[]{:S(2)}) copy-start(s32[1,512]{1,0:T(1,128)} %param.25) | copy-start | bytes 6148
  208.8 9.6 %all-to-all-start.4 = ((bf16[4,128,256]{2,1,0:T(8,128)(2,1)}), bf16[4,128,256]{2,1,0:T(8,128)(2,1)S(1)}, u32[]{:S(2)}, u32[]{:S(2)}) async-start(bf16[4,128,256]{2,1,0:T(8,128)(2,1)} %broadcast_select_fusion.1), calls=%async_computation.4 | async-start | bytes 524288 | tf_op jit(solution)/shard_map/all_to_all | solution.py:101
  218.4 8.8 %copy-start.5 = (bf16[4,128,256]{2,1,0:T(8,128)(2,1)}, bf16[4,128,256]{2,1,0:T(8,128)(2,1)S(1)}, u32[]{:S(2)}) copy-start(bf16[4,128,256]{2,1,0:T(8,128)(2,1)S(1)} %all-to-all-done.4) | copy-start | bytes 786436
  218.4 8.8 %all-to-all-start.1 = ((bf16[4,128,256]{2,1,0:T(8,128)(2,1)}), bf16[4,128,256]{2,1,0:T(8,128)(2,1)S(1)}, u32[]{:S(2)}, u32[]{:S(2)}) async-start(bf16[4,128,256]{2,1,0:T(8,128)(2,1)} %bitcast.19), calls=%async_computation.1 | async-start | bytes 524288 | tf_op jit(solution)/shard_map/all_to_all | solution.py:95
  227.1 18.8 %all-to-all-start.3 = ((bf16[8,128,256]{2,1,0:T(8,128)(2,1)}), bf16[8,128,256]{2,1,0:T(8,128)(2,1)S(1)}, u32[]{:S(2)}, u32[]{:S(2)}) async-start(bf16[8,128,256]{2,1,0:T(8,128)(2,1)} %bitcast.30), calls=%async_computation.3 | async-start | bytes 1048576 | tf_op jit(solution)/shard_map/all_to_all | solution.py:120
  243.7 6.5 %copy-start.6 = (bf16[4,128,256]{2,1,0:T(8,128)(2,1)S(1)}, bf16[4,128,256]{2,1,0:T(8,128)(2,1)}, u32[]{:S(2)}) copy-start(bf16[4,128,256]{2,1,0:T(8,128)(2,1)} %copy-done.5) | copy-start | bytes 786436
  243.7 73.2 %copy-start.9 = (f32[256]{0:T(256)S(1)}, f32[256]{0:T(256)}, u32[]{:S(2)}) copy-start(f32[256]{0:T(256)} %param.17) | copy-start | bytes 3076
  245.9 76.2 %all-to-all-start.5 = ((f32[8,128,256]{2,1,0:T(8,128)}), f32[8,128,256]{2,1,0:T(8,128)S(1)}, u32[]{:S(2)}, u32[]{:S(2)}) async-start(f32[8,128,256]{2,1,0:T(8,128)} %broadcast_select_fusion), calls=%async_computation.5 | async-start | bytes 2097152 | tf_op jit(solution)/shard_map/all_to_all | solution.py:134
  249.9 66.0 %all-reduce.3.cloned.1.call-start = ((), (), s32[]{:S(2)}) async-start(), calls=%async_computation.6 | async-start | bytes 524288 | tf_op jit(solution)/shard_map/psum | solution.py:103
  251.2 113.1 %all-reduce.5.cloned.1.call-start = ((), (), s32[]{:S(2)}) async-start(), calls=%async_computation.7 | async-start | bytes 262144 | tf_op jit(solution)/shard_map/psum | solution.py:138
Sparse Core Ops, SparseCore 0:
  253.6 62.2 all-reduce.2
Sparse Core Ops, SparseCore 1:
  323.5 40.7 all-reduce.4
where the time goes:
time: 375 us; the launch traced here: 373 us
  local copies, waits for them, and re-layouts  135 us (36%)
  waiting for transfers between devices  110 us (29%)
  matrix products  68.8 us (18%)
  starting transfers between devices  25.2 us (7%)
  other arithmetic  18 us (5%)
  between operations  15.8 us (4%)
    psum x1, waiting for transfers between devices, local(): total_grad = lax.psum(row_grad, 'tt')  63.3 us
    dot_general x4, matrix products, rank_one_block(): jnp.einsum('nawb,nbe->nawe', mid_cores, last_cores, preferred_element_typ...  57 us
    reshape x4, local copies, waits for them, and re-layouts, rank_one_block(): mid_cores = core_mid[mid_part].reshape(-1, RANK, E2, RANK)  46.9 us
    gather x8, local copies, waits for them, and re-layouts, rank_one_block(): mid_cores = core_mid[mid_part].reshape(-1, RANK, E2, RANK)  38.8 us
    psum x1, waiting for transfers between devices, local(): core_total = lax.psum(core_grad, 'hot')  35.9 us
    gather x4, local copies, waits for them, and re-layouts, packed(): return jnp.take(values, source, axis=0, mode='fill', fill_value=fill_value)  15.9 us
  transfers between devices with their start and end apart: 8, of which 6 were waited for; matrix products, arithmetic and copies ran while one was open for 56% of the time, Pallas kernels for 0%

commit v1 on v0

--- a/solution.py
+++ b/solution.py
@@ -100,7 +100,7 @@
     sending = packed(hot_cot, row_source, 0).reshape(hot_peers, hot_cap, feature_width)
     received = lax.all_to_all(sending, "hot", split_axis=0, concat_axis=0, tiled=True)
     row_grad = owner_sum(served.reshape(-1), received.reshape(-1, feature_width), rows_held, None)
-    total_grad = lax.psum(row_grad, "tt")
+    total_grad = jnp.sum(lax.all_gather(row_grad, "tt"), axis=0)
     new_table, new_accum = adagrad(hot_table, hot_accum, total_grad)
     slices_held = core_first.shape[0]
     tt_peers = lax.axis_size("tt")

time: 375 us -> 316 us (0.84)
  waiting for transfers between devices: 110 us -> 53.9 us
    psum x1 -> x0, waiting for transfers between devices: 63.3 us -> none  [local(): total_grad = lax.psum(row_grad, 'tt')]
    psum x1, waiting for transfers between devices: 35.9 us -> 0.01 us  [local(): core_total = lax.psum(core_grad, 'hot')]
    all_to_all x1, waiting for transfers between devices: 0.01 us -> 23.4 us  [local(): lax.all_to_all(grad_out, 'tt', split_axis=0, concat_axis=0, tiled=True)]
    all_to_all x1, waiting for transfers between devices: 1.02 us -> 21.3 us  [local(): back = lax.all_to_all(slices, 'tt', split_axis=0, concat_axis=0, tiled=True)]
  transfers between devices with their start and end apart: 8 -> 8, of which waited for: 6 -> 5; matrix products, arithmetic and copies ran while one was open for 56% -> 66% of each run, Pallas kernels for 0% -> 0%
where the time goes in v1:
time: 316 us; the launch traced here: 314 us
  local copies, waits for them, and re-layouts  133 us (42%)
  matrix products  68.5 us (22%)
  waiting for transfers between devices  53.9 us (17%)
  starting transfers between devices  24.8 us (8%)
  other arithmetic  17.9 us (6%)
  between operations  15.8 us (5%)
    dot_general x4, matrix products, rank_one_block(): jnp.einsum('nawb,nbe->nawe', mid_cores, last_cores, preferred_element_typ...  57 us
    reshape x4, local copies, waits for them, and re-layouts, rank_one_block(): mid_cores = core_mid[mid_part].reshape(-1, RANK, E2, RANK)  46.9 us
    gather x8, local copies, waits for them, and re-layouts, rank_one_block(): mid_cores = core_mid[mid_part].reshape(-1, RANK, E2, RANK)  38.8 us
    all_to_all x1, waiting for transfers between devices, local(): lax.all_to_all(grad_out, 'tt', split_axis=0, concat_axis=0, tiled=True)  23.4 us
    all_to_all x1, waiting for transfers between devices, local(): back = lax.all_to_all(slices, 'tt', split_axis=0, concat_axis=0, tiled=True)  21.3 us
    gather x4, local copies, waits for them, and re-layouts, packed(): return jnp.take(values, source, axis=0, mode='fill', fill_value=fill_value)  16.1 us
  transfers between devices with their start and end apart: 8, of which 5 were waited for; matrix products, arithmetic and copies ran while one was open for 66% of the time, Pallas kernels for 0%

profile of v1, /device:TPU:0, one launch (start us, length us, event | category | flops | bytes accessed | tf_op | source)
XLA Modules:
  0.0 314.1 jit_solution(1622539135402379654)
XLA Ops:
  8.7 1.2 reduce-window.14
  11.7 1.4 scatter_custom_fusion
  13.1 3.6 %gather_fusion.2 = s32[512]{0:T(512)S(1)} fusion(s32[256]{0:T(256)} %bitcast.108, s32[1024]{0:T(1024)S(1)} %pad_clamp_fusion.5), kind=kCustom, calls=%fused_computation.2 | custom fusion | bytes 6144 | tf_op jit(solution)/shard_map/jit(_take)/gather | solution.py:26
  17.3 5.2 %all-to-all-start = ((s32[4,1,128]{2,1,0:T(1,128)}), s32[4,1,128]{2,1,0:T(1,128)S(1)}, u32[]{:S(2)}, u32[]{:S(2)}) async-start(s32[4,1,128]{2,1,0:T(1,128)} %bitcast.17), calls=%async_computation | async-start | bytes 4096 | tf_op jit(solution)/shard_map/all_to_all | solution.py:93
  23.2 1.1 reduce-window.16
  26.1 2.6 scatter_custom_fusion.1
  28.7 154.8 %while.2 = (s32[]{:T(128)}, bf16[4,128,1024]{2,1,0:T(8,128)(2,1)S(1)}, s32[4,128]{1,0:T(4,128)}, bf16[64,8192]{1,0:T(8,128)(2,1)}, s32[4,128]{1,0:T(4,128)}, /*index=5*/bf16[64,128]{1,0:T(8,128)(2,1)}, s32[]{:T(128)}) while((s32[]{:T(128)}, bf16[4,128,1024]{2,1,0:T(8,128)(2,1)S(1)}, s32[4,128]{1,0:T(4,128)}, bf16[64,8192]{1,0:T(8,128)(2,1)}, ...), condition=%wide.region_9.10_spmd, body=%wide.region_8.9_spmd.sunk | while | flops 8522498 | bytes 16822392 | solution.py:59
  29.4 6.5 %gather_fusion = bf16[128,8192]{1,0:T(8,128)(2,1)} fusion(bf16[64,8192]{1,0:T(8,128)(2,1)} %get-tuple-element.145, s32[1024]{0:T(1024)S(1)} %pad_clamp_fusion.8), kind=kCustom, calls=%fused_computation.clone.1 | custom fusion | bytes 4194816 | tf_op jit(solution)/shard_map/while/body/eval_jaxpr/gather | solution.py:52
  35.9 3.2 %copy.55 = bf16[128,8192]{0,1:T(8,128)(2,1)S(1)} copy(bf16[128,8192]{1,0:T(8,128)(2,1)} %gather_fusion) | data formatting | bytes 4194304 | tf_op jit(solution)/shard_map/while/body/eval_jaxpr/gather | solution.py:52
  39.1 11.7 %copy.56 = bf16[128,32,8,32]{3,1,2,0:T(8,128)(2,1)} copy(bf16[128,32,8,32]{0,3,2,1:T(8,128)(2,1)S(1)} %bitcast.109) | data formatting | bytes 4194304 | tf_op jit(solution)/shard_map/while/body/eval_jaxpr/reshape | solution.py:52
  51.9 14.3 %convolution_convert_fusion.5 = bf16[128,32,8,4]{1,3,2,0:T(4,128)(2,1)S(1)} fusion(bf16[128,32,8,32]{3,1,2,0:T(8,128)(2,1)} %copy.56, bf16[128,32,4,1]{1,2,3,0:T(4,128)(2,1)S(1)} %copy.58), kind=kOutput, calls=%fused_computation.12.clone.1 | convolution fusion | flops 8519680 | bytes 2392064 | tf_op jit(solution)/shard_map/while/body/eval_jaxpr/nawb,nbe->nawe/dot_general | solution.py:54
  66.1 1.1 copy.59
  68.1 6.5 %gather_fusion = bf16[128,8192]{1,0:T(8,128)(2,1)} fusion(bf16[64,8192]{1,0:T(8,128)(2,1)} %get-tuple-element.145, s32[1024]{0:T(1024)S(1)} %pad_clamp_fusion.8), kind=kCustom, calls=%fused_computation.clone.1 | custom fusion | bytes 4194816 | tf_op jit(solution)/shard_map/while/body/eval_jaxpr/gather | solution.py:52
  74.6 3.2 %copy.55 = bf16[128,8192]{0,1:T(8,128)(2,1)S(1)} copy(bf16[128,8192]{1,0:T(8,128)(2,1)} %gather_fusion) | data formatting | bytes 4194304 | tf_op jit(solution)/shard_map/while/body/eval_jaxpr/gather | solution.py:52
  77.8 11.7 %copy.56 = bf16[128,32,8,32]{3,1,2,0:T(8,128)(2,1)} copy(bf16[128,32,8,32]{0,3,2,1:T(8,128)(2,1)S(1)} %bitcast.109) | data formatting | bytes 4194304 | tf_op jit(solution)/shard_map/while/body/eval_jaxpr/reshape | solution.py:52
  90.6 14.3 %convolution_convert_fusion.5 = bf16[128,32,8,4]{1,3,2,0:T(4,128)(2,1)S(1)} fusion(bf16[128,32,8,32]{3,1,2,0:T(8,128)(2,1)} %copy.56, bf16[128,32,4,1]{1,2,3,0:T(4,128)(2,1)S(1)} %copy.58), kind=kOutput, calls=%fused_computation.12.clone.1 | convolution fusion | flops 8519680 | bytes 2392064 | tf_op jit(solution)/shard_map/while/body/eval_jaxpr/nawb,nbe->nawe/dot_general | solution.py:54
  104.8 1.1 copy.59
  106.8 6.5 %gather_fusion = bf16[128,8192]{1,0:T(8,128)(2,1)} fusion(bf16[64,8192]{1,0:T(8,128)(2,1)} %get-tuple-element.145, s32[1024]{0:T(1024)S(1)} %pad_clamp_fusion.8), kind=kCustom, calls=%fused_computation.clone.1 | custom fusion | bytes 4194816 | tf_op jit(solution)/shard_map/while/body/eval_jaxpr/gather | solution.py:52
  113.3 3.2 %copy.55 = bf16[128,8192]{0,1:T(8,128)(2,1)S(1)} copy(bf16[128,8192]{1,0:T(8,128)(2,1)} %gather_fusion) | data formatting | bytes 4194304 | tf_op jit(solution)/shard_map/while/body/eval_jaxpr/gather | solution.py:52
  116.5 11.7 %copy.56 = bf16[128,32,8,32]{3,1,2,0:T(8,128)(2,1)} copy(bf16[128,32,8,32]{0,3,2,1:T(8,128)(2,1)S(1)} %bitcast.109) | data formatting | bytes 4194304 | tf_op jit(solution)/shard_map/while/body/eval_jaxpr/reshape | solution.py:52
  129.3 14.3 %convolution_convert_fusion.5 = bf16[128,32,8,4]{1,3,2,0:T(4,128)(2,1)S(1)} fusion(bf16[128,32,8,32]{3,1,2,0:T(8,128)(2,1)} %copy.56, bf16[128,32,4,1]{1,2,3,0:T(4,128)(2,1)S(1)} %copy.58), kind=kOutput, calls=%fused_computation.12.clone.1 | convolution fusion | flops 8519680 | bytes 2392064 | tf_op jit(solution)/shard_map/while/body/eval_jaxpr/nawb,nbe->nawe/dot_general | solution.py:54
  145.5 6.5 %gather_fusion = bf16[128,8192]{1,0:T(8,128)(2,1)} fusion(bf16[64,8192]{1,0:T(8,128)(2,1)} %get-tuple-element.145, s32[1024]{0:T(1024)S(1)} %pad_clamp_fusion.8), kind=kCustom, calls=%fused_computation.clone.1 | custom fusion | bytes 4194816 | tf_op jit(solution)/shard_map/while/body/eval_jaxpr/gather | solution.py:52
  152.0 3.2 %copy.55 = bf16[128,8192]{0,1:T(8,128)(2,1)S(1)} copy(bf16[128,8192]{1,0:T(8,128)(2,1)} %gather_fusion) | data formatting | bytes 4194304 | tf_op jit(solution)/shard_map/while/body/eval_jaxpr/gather | solution.py:52
  155.2 11.7 %copy.56 = bf16[128,32,8,32]{3,1,2,0:T(8,128)(2,1)} copy(bf16[128,32,8,32]{0,3,2,1:T(8,128)(2,1)S(1)} %bitcast.109) | data formatting | bytes 4194304 | tf_op jit(solution)/shard_map/while/body/eval_jaxpr/reshape | solution.py:52
  168.0 14.3 %convolution_convert_fusion.5 = bf16[128,32,8,4]{1,3,2,0:T(4,128)(2,1)S(1)} fusion(bf16[128,32,8,32]{3,1,2,0:T(8,128)(2,1)} %copy.56, bf16[128,32,4,1]{1,2,3,0:T(4,128)(2,1)S(1)} %copy.58), kind=kOutput, calls=%fused_computation.12.clone.1 | convolution fusion | flops 8519680 | bytes 2392064 | tf_op jit(solution)/shard_map/while/body/eval_jaxpr/nawb,nbe->nawe/dot_general | solution.py:54
  183.5 4.4 %reshape.358 = bf16[512,32,32]{2,1,0:T(8,128)(2,1)} reshape(bf16[4,128,1024]{2,1,0:T(8,128)(2,1)S(1)} %get-tuple-element.66) | data formatting | bytes 2097152 | tf_op jit(solution)/shard_map/reshape;reshape | solution.py:122
  189.0 7.1 %gather_fusion.5 = s32[1024]{0:T(1024)S(1)} fusion(s32[512]{0:T(512)S(1)} %bitcast.107, s32[1024]{0:T(1024)S(1)} %fusion.18), kind=kCustom, calls=%fused_computation.5 | custom fusion | bytes 12288 | tf_op jit(solution)/shard_map/jit(_take)/gather | solution.py:26
  196.1 4.4 %fusion.25 = f32[512,8,32]{2,1,0:T(8,128)S(1)} fusion(bf16[512,8,32]{2,1,0:T(8,128)(2,1)S(1)} %copy.36, bf16[512,32,32]{2,1,0:T(8,128)(2,1)} %reshape.358), kind=kOutput, calls=%fused_computation.83 | convolution fusion | flops 8388608 | bytes 1835008 | tf_op jit(solution)/shard_map/kej,kaj->kea/dot_general | solution.py:125
  202.1 3.5 %gather_fusion.9 = f32[1024,256]{1,0:T(8,128)S(1)} fusion(f32[512,256]{1,0:T(8,128)S(1)} %copy.39, s32[1024]{0:T(1024)S(1)} %fusion.18), kind=kCustom, calls=%fused_computation.9 | custom fusion | bytes 2101248 | tf_op jit(solution)/shard_map/jit(_take)/gather | solution.py:26
  205.6 4.9 %all-to-all-start.2 = ((s32[8,1,128]{2,1,0:T(1,128)}), s32[8,1,128]{2,1,0:T(1,128)S(1)}, u32[]{:S(2)}, u32[]{:S(2)}) async-start(s32[8,1,128]{2,1,0:T(1,128)} %bitcast.28), calls=%async_computation.2 | async-start | bytes 8192 | tf_op jit(solution)/shard_map/all_to_all | solution.py:118
  210.5 1.2 broadcast_select_fusion
  211.6 4.3 %all-to-all-done.2 = s32[8,1,128]{2,1,0:T(1,128)S(1)} async-done(((s32[8,1,128]{2,1,0:T(1,128)}), s32[8,1,128]{2,1,0:T(1,128)S(1)}, u32[]{:S(2)}, u32[]{:S(2)}) %all-to-all-start.2) | async-done | bytes 4128 | tf_op jit(solution)/shard_map/all_to_all | solution.py:118
  216.0 3.6 %all-to-all-start.5 = ((f32[8,128,256]{2,1,0:T(8,128)}), f32[8,128,256]{2,1,0:T(8,128)S(1)}, u32[]{:S(2)}, u32[]{:S(2)}) async-start(f32[8,128,256]{2,1,0:T(8,128)} %broadcast_select_fusion), calls=%async_computation.5 | async-start | bytes 2097152 | tf_op jit(solution)/shard_map/all_to_all | solution.py:134
  219.8 2.0 gather_fusion.8
  222.6 23.4 %all-to-all-done.5 = f32[8,128,256]{2,1,0:T(8,128)S(1)} async-done(((f32[8,128,256]{2,1,0:T(8,128)}), f32[8,128,256]{2,1,0:T(8,128)S(1)}, u32[]{:S(2)}, u32[]{:S(2)}) %all-to-all-start.5) | async-done | bytes 1048608 | tf_op jit(solution)/shard_map/all_to_all | solution.py:134
  246.0 4.2 %all-to-all-start.4 = ((bf16[4,128,256]{2,1,0:T(8,128)(2,1)}), bf16[4,128,256]{2,1,0:T(8,128)(2,1)S(1)}, u32[]{:S(2)}, u32[]{:S(2)}) async-start(bf16[4,128,256]{2,1,0:T(8,128)(2,1)} %broadcast_select_fusion.1), calls=%async_computation.4 | async-start | bytes 524288 | tf_op jit(solution)/shard_map/all_to_all | solution.py:101
  250.2 1.2 fusion.5
  251.5 4.1 %all-to-all-done.4 = bf16[4,128,256]{2,1,0:T(8,128)(2,1)S(1)} async-done(((bf16[4,128,256]{2,1,0:T(8,128)(2,1)}), bf16[4,128,256]{2,1,0:T(8,128)(2,1)S(1)}, u32[]{:S(2)}, u32[]{:S(2)}) %all-to-all-start.4) | async-done | bytes 262176 | tf_op jit(solution)/shard_map/all_to_all | solution.py:101
  256.6 2.2 gather_fusion.3
  258.8 3.4 %all-to-all-start.1 = ((bf16[4,128,256]{2,1,0:T(8,128)(2,1)}), bf16[4,128,256]{2,1,0:T(8,128)(2,1)S(1)}, u32[]{:S(2)}, u32[]{:S(2)}) async-start(bf16[4,128,256]{2,1,0:T(8,128)(2,1)} %bitcast.19), calls=%async_computation.1 | async-start | bytes 524288 | tf_op jit(solution)/shard_map/all_to_all | solution.py:95
  262.3 4.6 %gather_fusion.6 = bf16[1024,256]{1,0:T(8,128)(2,1)} fusion(f32[128,256]{1,0:T(8,128)S(1)} %copy-done.2, s32[1024]{0:T(1024)S(1)} %broadcast_clamp_fusion), kind=kCustom, calls=%fused_computation.6 | custom fusion | bytes 1052672 | tf_op jit(solution)/shard_map/gather | solution.py:119
  267.6 3.5 %all-to-all-start.3 = ((bf16[8,128,256]{2,1,0:T(8,128)(2,1)}), bf16[8,128,256]{2,1,0:T(8,128)(2,1)S(1)}, u32[]{:S(2)}, u32[]{:S(2)}) async-start(bf16[8,128,256]{2,1,0:T(8,128)(2,1)} %bitcast.30), calls=%async_computation.3 | async-start | bytes 1048576 | tf_op jit(solution)/shard_map/all_to_all | solution.py:120
  271.4 1.2 gather_fusion.4
  272.6 21.3 %all-to-all-done.3 = bf16[8,128,256]{2,1,0:T(8,128)(2,1)S(1)} async-done(((bf16[8,128,256]{2,1,0:T(8,128)(2,1)}), bf16[8,128,256]{2,1,0:T(8,128)(2,1)S(1)}, u32[]{:S(2)}, u32[]{:S(2)}) %all-to-all-start.3) | async-done | bytes 524320 | tf_op jit(solution)/shard_map/all_to_all | solution.py:120
  293.9 1.9 gather_fusion.7
  296.8 3.4 %convolution_convert_fusion.1 = bf16[512,8,32]{2,1,0:T(8,128)(2,1)S(1)} fusion(bf16[512,8,32]{2,1,0:T(8,128)(2,1)S(1)} %copy.32, bf16[512,32,32]{2,1,0:T(8,128)(2,1)} %reshape.358), kind=kOutput, calls=%fused_computation.24 | convolution fusion | flops 8519680 | bytes 1572864 | tf_op jit(solution)/shard_map/kea,kaj->kej/dot_general | solution.py:123
  301.8 1.6 multiply_subtract_fusion
  303.4 1.8 reduce_sum.44
  (110 shorter events, 25.0 us)
Async XLA Ops:
  8.0 179.9 %copy-start = (bf16[64,256]{1,0:T(8,128)(2,1)S(1)}, bf16[64,256]{1,0:T(8,128)(2,1)}, u32[]{:S(2)}) copy-start(bf16[64,256]{1,0:T(8,128)(2,1)} %param.29) | copy-start | bytes 98308
  17.3 188.2 %all-to-all-start = ((s32[4,1,128]{2,1,0:T(1,128)}), s32[4,1,128]{2,1,0:T(1,128)S(1)}, u32[]{:S(2)}, u32[]{:S(2)}) async-start(s32[4,1,128]{2,1,0:T(1,128)} %bitcast.17), calls=%async_computation | async-start | bytes 4096 | tf_op jit(solution)/shard_map/all_to_all | solution.py:93
  39.1 11.7 %copy-start.3 = (bf16[64,128]{1,0:T(8,128)(2,1)S(1)}, bf16[64,128]{1,0:T(8,128)(2,1)}, u32[]{:S(2)}) copy-start(bf16[64,128]{1,0:T(8,128)(2,1)} %get-tuple-element.147) | copy-start | bytes 49156 | tf_op jit(solution)/shard_map/while
  77.8 11.7 %copy-start.3 = (bf16[64,128]{1,0:T(8,128)(2,1)S(1)}, bf16[64,128]{1,0:T(8,128)(2,1)}, u32[]{:S(2)}) copy-start(bf16[64,128]{1,0:T(8,128)(2,1)} %get-tuple-element.147) | copy-start | bytes 49156 | tf_op jit(solution)/shard_map/while
  116.5 11.7 %copy-start.3 = (bf16[64,128]{1,0:T(8,128)(2,1)S(1)}, bf16[64,128]{1,0:T(8,128)(2,1)}, u32[]{:S(2)}) copy-start(bf16[64,128]{1,0:T(8,128)(2,1)} %get-tuple-element.147) | copy-start | bytes 49156 | tf_op jit(solution)/shard_map/while
  155.2 11.7 %copy-start.3 = (bf16[64,128]{1,0:T(8,128)(2,1)S(1)}, bf16[64,128]{1,0:T(8,128)(2,1)}, u32[]{:S(2)}) copy-start(bf16[64,128]{1,0:T(8,128)(2,1)} %get-tuple-element.147) | copy-start | bytes 49156 | tf_op jit(solution)/shard_map/while
  183.5 4.4 %copy-start.5 = (s32[1,512]{1,0:T(1,128)S(1)}, s32[1,512]{1,0:T(1,128)}, u32[]{:S(2)}) copy-start(s32[1,512]{1,0:T(1,128)} %param.25) | copy-start | bytes 6148
  183.5 5.5 %copy-start.1 = (s32[1,512]{1,0:T(1,128)S(1)}, s32[1,512]{1,0:T(1,128)}, u32[]{:S(2)}) copy-start(s32[1,512]{1,0:T(1,128)} %param.22) | copy-start | bytes 6148
  205.6 14.0 %copy-start.6 = (s32[1,256]{1,0:T(1,128)S(1)}, s32[1,256]{1,0:T(1,128)}, u32[]{:S(2)}) copy-start(s32[1,256]{1,0:T(1,128)} %param.20) | copy-start | bytes 3076
  205.6 10.4 %all-to-all-start.2 = ((s32[8,1,128]{2,1,0:T(1,128)}), s32[8,1,128]{2,1,0:T(1,128)S(1)}, u32[]{:S(2)}, u32[]{:S(2)}) async-start(s32[8,1,128]{2,1,0:T(1,128)} %bitcast.28), calls=%async_computation.2 | async-start | bytes 8192 | tf_op jit(solution)/shard_map/all_to_all | solution.py:118
  211.6 45.0 %copy-start.4 = (f32[256,256]{1,0:T(8,128)S(1)}, f32[256,256]{1,0:T(8,128)}, u32[]{:S(2)}) copy-start(f32[256,256]{1,0:T(8,128)} %param.16) | copy-start | bytes 786436
  216.0 30.1 %all-to-all-start.5 = ((f32[8,128,256]{2,1,0:T(8,128)}), f32[8,128,256]{2,1,0:T(8,128)S(1)}, u32[]{:S(2)}, u32[]{:S(2)}) async-start(f32[8,128,256]{2,1,0:T(8,128)} %broadcast_select_fusion), calls=%async_computation.5 | async-start | bytes 2097152 | tf_op jit(solution)/shard_map/all_to_all | solution.py:134
  219.8 42.5 %copy-start.2 = (f32[128,256]{1,0:T(8,128)S(1)}, f32[128,256]{1,0:T(8,128)}, u32[]{:S(2)}) copy-start(f32[128,256]{1,0:T(8,128)} %param.26) | copy-start | bytes 393220
  246.0 9.6 %all-to-all-start.4 = ((bf16[4,128,256]{2,1,0:T(8,128)(2,1)}), bf16[4,128,256]{2,1,0:T(8,128)(2,1)S(1)}, u32[]{:S(2)}, u32[]{:S(2)}) async-start(bf16[4,128,256]{2,1,0:T(8,128)(2,1)} %broadcast_select_fusion.1), calls=%async_computation.4 | async-start | bytes 524288 | tf_op jit(solution)/shard_map/all_to_all | solution.py:101
  250.2 51.5 %all-reduce.2.cloned.1.call-start = ((), (), s32[]{:S(2)}) async-start(), calls=%async_computation.6 | async-start | bytes 262144 | tf_op jit(solution)/shard_map/psum | solution.py:138
  251.5 51.9 %all-gather.3.cloned.1.call-start = ((), (), s32[]{:S(2)}) async-start(), calls=%async_computation.7 | async-start | bytes 2359296 | tf_op jit(solution)/shard_map/all_gather | solution.py:103
  258.8 8.8 %all-to-all-start.1 = ((bf16[4,128,256]{2,1,0:T(8,128)(2,1)}), bf16[4,128,256]{2,1,0:T(8,128)(2,1)S(1)}, u32[]{:S(2)}, u32[]{:S(2)}) async-start(bf16[4,128,256]{2,1,0:T(8,128)(2,1)} %bitcast.19), calls=%async_computation.1 | async-start | bytes 524288 | tf_op jit(solution)/shard_map/all_to_all | solution.py:95
  267.6 26.3 %all-to-all-start.3 = ((bf16[8,128,256]{2,1,0:T(8,128)(2,1)}), bf16[8,128,256]{2,1,0:T(8,128)(2,1)S(1)}, u32[]{:S(2)}, u32[]{:S(2)}) async-start(bf16[8,128,256]{2,1,0:T(8,128)(2,1)} %bitcast.30), calls=%async_computation.3 | async-start | bytes 1048576 | tf_op jit(solution)/shard_map/all_to_all | solution.py:120
  300.1 5.1 %copy-start.7 = (f32[256]{0:T(256)S(1)}, f32[256]{0:T(256)}, u32[]{:S(2)}) copy-start(f32[256]{0:T(256)} %param.17) | copy-start | bytes 3076
Sparse Core Ops, SparseCore 0:
  254.5 41.5 all-reduce.1
Sparse Core Ops, SparseCore 1:
  256.7 36.8 all-gather.2
